TPU v7x, 256 devices: a whole 4x4x8 slice. The times are simulated.
256 devices in a mesh: video: 4 (over x), tm: 16 (over z, core), space: 4 (over y).
Axes of the slice: x: 4, y: 4, z: 8, core: 2. Of those that a mesh axis runs over, the one named last changes fastest.
Arguments:
- feature_maps: bfloat16 [64, 128, 240, 128], P(('video', 'tm'), 'space'), parts along dimension 0, may hold values from -27 to 27
- query_frame: int32 [2048], P('video'), parts along dimension 0, may hold values from 0 to 15
- query_row: int32 [2048], P('video'), parts along dimension 0, may hold values from 0 to 127
- query_col: int32 [2048], P('video'), parts along dimension 0, may hold values from 0 to 239
- ema_decay: float32 [64, 128], P(('video', 'tm')), parts along dimension 0, may hold values from 0.14 to 1
- dw_kernel: float32 [3, 128], replicated, may hold values from -3 to 3
- pw_weight: bfloat16 [128, 128], replicated, may hold values from -0.5 to 0.5
- out_weight: float32 [2, 128], replicated, may hold values from -2 to 2
Outputs:
- tracks: float32 [64, 2, 512], P(('video', 'tm')), parts along dimension 0
There are 4 independent parts, one for each index of `video`. A program takes and returns all parts, laid end to end along the dimension named above; an argument that names none is the same for every part. Nothing has to cross between parts.
All inputs are finite; a program needn't handle non-finite values.
Results may differ from a plain program's by a relative error of at most 0.0026.
Values may be sent and summed in bfloat16 or wider, within the bound.
A program may use at most 128 MiB of HBM per device.

v0:
```python
import math
import jax
import jax.numpy as jnp
from jax import lax
from jax.sharding import PartitionSpec as P


def with_halo(cells, sides, width):
    for axis, dim in sides:
        count = lax.axis_size(axis)
        ends = count - 1
        head = lax.slice_in_dim(cells, 0, width, axis=dim)
        tail = lax.slice_in_dim(cells, cells.shape[dim] - width, cells.shape[dim], axis=dim)
        cells = jnp.concatenate(
            [
                lax.ppermute(tail, axis, [(i, (i + 1) % count) for i in range(ends)]),
                cells,
                lax.ppermute(head, axis, [((i + 1) % count, i) for i in range(ends)]),
            ],
            axis=dim,
        )
    return cells


def local(
    feature_maps, query_frame, query_row, query_col, ema_decay, dw_kernel, pw_weight, out_weight
):
    frames_here, rows_here, map_width, channels = feature_maps.shape
    num_queries = query_frame.shape[0]
    first_frame = lax.axis_index("tm") * frames_here
    first_row = lax.axis_index("space") * rows_here
    map_height = rows_here * lax.axis_size("space")
    local_frame = query_frame - first_frame
    local_row = query_row - first_row
    owned = (
        (local_frame >= 0)
        & (local_frame < frames_here)
        & (local_row >= 0)
        & (local_row < rows_here)
    )
    picked = feature_maps[
        jnp.clip(local_frame, 0, frames_here - 1), jnp.clip(local_row, 0, rows_here - 1), query_col
    ]
    contrib = jnp.where(owned[:, None], picked.astype(jnp.float32), 0.0)
    query_feats = lax.psum(contrib, ("tm", "space")).astype(jnp.bfloat16)
    scale = 1.0 / math.sqrt(channels)
    col_coord = jnp.arange(map_width, dtype=jnp.int32).astype(jnp.float32) / map_width
    row_coord = (first_row + jnp.arange(rows_here, dtype=jnp.int32)).astype(
        jnp.float32
    ) / map_height
    highest_list, total_list, pos_list, feat_list = ([], [], [], [])
    frame_index = 0
    frame_map = feature_maps[frame_index].reshape(rows_here * map_width, channels)
    scores = (
        lax.dot_general(
            query_feats, frame_map, (((1,), (1,)), ((), ())), preferred_element_type=jnp.float32
        )
        * scale
    )
    highest = jnp.max(scores, axis=1)
    weights_exp = jnp.exp(scores - highest[:, None])
    highest_list.append(highest)
    total_list.append(jnp.sum(weights_exp, axis=1))
    grid = weights_exp.reshape(num_queries, rows_here, map_width)
    col_part = jnp.sum(jnp.sum(grid, axis=1) * col_coord[None, :], axis=1)
    line_portion = jnp.sum(jnp.sum(grid, axis=2) * row_coord[None, :], axis=1)
    pos_list.append(jnp.stack([col_part, line_portion], 1))
    feat_list.append(
        jnp.dot(weights_exp.astype(jnp.bfloat16), frame_map, preferred_element_type=jnp.float32)
    )
    highest = jnp.stack(highest_list)
    totals = jnp.stack(total_list)
    pos_sum = jnp.stack(pos_list)
    feat_sum = jnp.stack(feat_list)
    top_value = lax.pmax(highest, "space")
    factor = jnp.exp(highest - top_value)
    grand_total, pos_all, feat_all = lax.psum(
        (factor * totals, factor[..., None] * pos_sum, factor[..., None] * feat_sum), "space"
    )
    position = pos_all / grand_total[..., None]
    focused_result = (feat_all / grand_total[..., None]).astype(jnp.bfloat16)
    padded = with_halo(focused_result, (("tm", 0),), 1).astype(jnp.float32)
    depth = jnp.zeros((frames_here, num_queries, channels), jnp.float32)
    for tap in range(dw_kernel.shape[0]):
        depth = depth + dw_kernel[tap][None, None, :] * padded[tap : tap + frames_here]
    hidden = jax.nn.gelu(depth).astype(jnp.bfloat16)
    mixed = jnp.dot(
        hidden.reshape(-1, channels), pw_weight, preferred_element_type=jnp.float32
    ).reshape(frames_here, num_queries, channels)
    refined = focused_result.astype(jnp.float32) + mixed
    carried = jnp.zeros((num_queries, channels), jnp.float32)
    retain_prod = jnp.ones((channels,), jnp.float32)
    local_states, local_prods = ([], [])
    frame_index = 0
    retain = ema_decay[frame_index]
    carried = retain[None, :] * carried + (1.0 - retain[None, :]) * refined[frame_index]
    retain_prod = retain_prod * retain
    local_states.append(carried)
    local_prods.append(retain_prod)
    all_prods, all_ends = (
        lax.all_gather(retain_prod[None], "tm", axis=0, tiled=True),
        lax.all_gather(carried[None], "tm", axis=0, tiled=True),
    )
    position_tm = lax.axis_index("tm")

    def fold_step(source, running):
        advanced = all_prods[source][None, :] * running + all_ends[source]
        return jnp.where(source < position_tm, advanced, running)

    incoming = lax.fori_loop(
        0, lax.axis_size("tm"), fold_step, jnp.zeros((num_queries, channels), jnp.float32)
    )
    memory = jnp.stack(local_states) + jnp.stack(local_prods)[:, None, :] * incoming[None]
    delta = jnp.einsum("tqc,kc->tkq", memory, out_weight, precision=lax.Precision.HIGHEST)
    return jnp.transpose(position, (0, 2, 1)) + delta


def solution(mesh):
    placed = (
        P(("video", "tm"), "space", None, None),
        P("video"),
        P("video"),
        P("video"),
        P(("video", "tm"), None),
        P(),
        P(),
        P(),
    )
    return jax.shard_map(
        local, mesh=mesh, in_specs=placed, out_specs=P(("video", "tm"), None, None), check_vma=False
    )
```

profile of v0, /device:TPU:1, one launch (start us, length us, event | category | flops | bytes accessed | tf_op | source)
XLA Modules:
  0.0 416.0 jit_solution(9454271297745757524)
XLA Ops:
  8.1 3.1 gather_fusion
  11.4 250.4 %all-reduce.5 = bf16[512,128]{1,0:T(8,128)(2,1)S(1)} all-reduce(f32[512,128]{1,0:T(8,128)S(1)} %convert_select_fusion), channel_id=1, replica_groups=mesh['video'=4,'tm'=16,'space'=4] {'tm','space'}, use_global_device_ids=true, to_apply=%region_0.1 | all-reduce | flops 65536 | bytes 393216 | tf_op jit(solution)/shard_map/psum | solution.py:45
  261.8 2.3 multiply_reduce_fusion
  264.1 7.0 %fusion.50 = (f32[512]{0:T(512)S(1)}, f32[512,7680]{1,0:T(8,128)}) fusion(f32[512]{0:T(512)S(1)} %get-tuple-element.139, f32[512,7680]{1,0:T(8,128)S(1)} %get-tuple-element.140), kind=kLoop, calls=%fused_computation.74 | loop fusion | flops 11795968 | bytes 31461376 | tf_op jit(solution)/shard_map/reduce_sum | solution.py:63
  271.1 6.0 %pmax.7 = f32[1,512]{1,0:T(1,128)S(1)} all-reduce(f32[1,512]{1,0:T(1,128)S(1)} %bitcast.66), channel_id=1, replica_groups=mesh['video'=4,'tm'=16,'space'=4] {'space'}, use_global_device_ids=true, to_apply=%region_2.3 | all-reduce | flops 512 | bytes 4096 | tf_op jit(solution)/shard_map/pmax | solution.py:75
  277.1 8.4 %fusion.7 = f32[1,512,128]{2,1,0:T(8,128)} fusion(bf16[7680,128]{1,0:T(8,128)(2,1)S(1)} %bitcast.62, f32[512,7680]{1,0:T(8,128)} %get-tuple-element.135, f32[512]{0:T(512)S(1)} %bitcast.64), kind=kOutput, calls=%fused_computation.11 | convolution fusion | flops 1010630656 | bytes 17958912 | tf_op jit(solution)/shard_map/dot_general | solution.py:69
  285.5 15.7 %copy.10 = f32[512,7680]{0,1:T(8,128)} copy(f32[512,7680]{1,0:T(8,128)} %get-tuple-element.135) | data formatting | bytes 31457280 | tf_op jit(solution)/shard_map/exp | solution.py:61
  301.3 7.9 %fusion.48 = (f32[512,240]{0,1:T(8,128)S(1)}, f32[512,32]{0,1:T(8,128)S(1)}) fusion(f32[512,32,240]{0,2,1:T(8,128)} %bitcast.63), kind=kLoop, calls=%fused_computation.72 | loop fusion | flops 7725056 | bytes 16285696 | tf_op jit(solution)/shard_map/reduce_sum | solution.py:65
  309.4 7.5 %all-reduce = (f32[512]{0:T(512)S(1)}, f32[1,512,2]{1,2,0:T(2,128)S(1)}) all-reduce(f32[512]{0:T(512)S(1)} %bitcast.70, f32[1,512,2]{1,2,0:T(2,128)S(1)} %maximum_multiply_fusion), channel_id=1, replica_groups=mesh['video'=4,'tm'=16,'space'=4] {'space'}, use_global_device_ids=true, to_apply=%region_9.10 | all-reduce | flops 1536 | bytes 12288 | tf_op jit(solution)/shard_map/psum | solution.py:77
  317.0 15.6 %all-reduce.4.cloned.1.call-done = f32[1,512,128]{2,1,0:T(8,128)} async-done(((f32[1,512,128]{2,1,0:T(8,128)}), f32[1,512,128]{2,1,0:T(8,128)}) %all-reduce.4.cloned.1.call-update) | async-done | bytes 262160 | tf_op jit(solution)/shard_map/psum | solution.py:77
  333.7 4.7 %collective-permute-start.1 = (bf16[1,512,128]{2,1,0:T(8,128)(2,1)S(1)}, bf16[1,512,128]{2,1,0:T(8,128)(2,1)S(1)}, u32[]{:S(2)}, u32[]{:S(2)}) collective-permute-start(bf16[1,512,128]{2,1,0:T(8,128)(2,1)S(1)} %divide_convert_fusion), channel_id=1, source_target_pairs={{4,0},{8,4},{12,8},{16,12},{20,16},{24,20},{28,24},{32,28},{36,32}... | collective-permute-start | bytes 393224 | tf_op jit(solution)/shard_map/ppermute | solution.py:18
  338.4 3.1 collective-permute-start
  342.2 1.2 collective-permute-done
  344.5 18.6 %all-gather = f32[16,1,128]{2,1,0:T(1,128)S(1)} all-gather(f32[1,1,128]{2,1,0:T(1,128)S(1)} %bitcast.73), channel_id=1, replica_groups=mesh['video'=4,'tm'=16,'space'=4] {'tm'}, dimensions={0}, use_global_device_ids=true | all-gather | bytes 8704 | tf_op jit(solution)/shard_map/all_gather | solution.py:101
  363.0 26.2 %all-gather.3.cloned.1.call-done = f32[16,512,128]{2,1,0:T(8,128)} async-done(((f32[1,512,128]{2,1,0:T(8,128)}), f32[16,512,128]{2,1,0:T(8,128)}) %all-gather.3.cloned.1.call-update) | async-done | bytes 4194320 | tf_op jit(solution)/shard_map/all_gather | solution.py:102
  389.2 19.0 %while.14 = (s32[]{:T(128)}, f32[512,128]{1,0:T(8,128)S(1)}, s32[]{:T(128)}, f32[16,128]{1,0:T(8,128)S(1)}, f32[16,512,128]{2,1,0:T(8,128)}, /*index=5*/s32[]{:T(128)}, s32[]{:T(128)}) while((s32[]{:T(128)}, f32[512,128]{1,0:T(8,128)S(1)}, s32[]{:T(128)}, f32[16,128]{1,0:T(8,128)S(1)}, f32[16,512,128]{2,1,0:T(8,128)}, ...), condition=%wide.region_12.13_spmd.clone, body=%wide.region_11.12_spmd.clone.sunk | while | flops 262148 | bytes 788081 | solution.py:110
  389.2 1.1 fusion.57
  390.4 1.1 fusion.57
  391.6 1.1 fusion.57
  392.8 1.1 fusion.57
  394.0 1.1 fusion.57
  395.1 1.1 fusion.57
  396.3 1.1 fusion.57
  397.5 1.1 fusion.57
  398.7 1.1 fusion.57
  399.9 1.1 fusion.57
  401.1 1.1 fusion.57
  402.3 1.1 fusion.57
  403.5 1.1 fusion.57
  404.7 1.1 fusion.57
  405.9 1.1 fusion.57
  407.0 1.1 fusion.57
  (48 shorter events, 6.0 us)
Async XLA Ops:
  6.5 1.6 copy-start
  6.5 326.1 %all-reduce.4.cloned.1.call-start = ((), (), s32[]{:S(2)}) async-start(), calls=%async_computation | async-start | bytes 524288 | tf_op jit(solution)/shard_map/psum | solution.py:77
  285.5 103.7 %all-gather.3.cloned.1.call-start = ((), (), s32[]{:S(2)}) async-start(), calls=%async_computation.1 | async-start | bytes 4456448 | tf_op jit(solution)/shard_map/all_gather | solution.py:102
  301.3 8.1 %copy-start.1 = (f32[1,128]{1,0:T(1,128)S(1)}, f32[1,128]{1,0:T(1,128)}, u32[]{:S(2)}) copy-start(f32[1,128]{1,0:T(1,128)} %param.14) | copy-start | bytes 1540
  301.3 15.7 %copy-start.2 = (f32[3,128]{1,0:T(4,128)S(1)}, f32[3,128]{1,0:T(4,128)}, u32[]{:S(2)}) copy-start(f32[3,128]{1,0:T(4,128)} %param.15) | copy-start | bytes 4612
  301.3 42.2 %copy-start.4 = (bf16[128,128]{1,0:T(8,128)(2,1)S(1)}, bf16[128,128]{1,0:T(8,128)(2,1)}, u32[]{:S(2)}) copy-start(bf16[128,128]{1,0:T(8,128)(2,1)} %param.16) | copy-start | bytes 98308
  301.3 106.9 %copy-start.3 = (f32[2,128]{1,0:T(2,128)S(1)}, f32[2,128]{1,0:T(2,128)}, u32[]{:S(2)}) copy-start(f32[2,128]{1,0:T(2,128)} %param.17) | copy-start | bytes 3076
  333.7 8.5 %collective-permute-start.1 = (bf16[1,512,128]{2,1,0:T(8,128)(2,1)S(1)}, bf16[1,512,128]{2,1,0:T(8,128)(2,1)S(1)}, u32[]{:S(2)}, u32[]{:S(2)}) collective-permute-start(bf16[1,512,128]{2,1,0:T(8,128)(2,1)S(1)} %divide_convert_fusion), channel_id=1, source_target_pairs={{4,0},{8,4},{12,8},{16,12},{20,16},{24,20},{28,24},{32,28},{36,32}... | collective-permute-start | bytes 393224 | tf_op jit(solution)/shard_map/ppermute | solution.py:18
  338.4 5.0 %collective-permute-start = (bf16[1,512,128]{2,1,0:T(8,128)(2,1)S(1)}, bf16[1,512,128]{2,1,0:T(8,128)(2,1)S(1)}, u32[]{:S(2)}, u32[]{:S(2)}) collective-permute-start(bf16[1,512,128]{2,1,0:T(8,128)(2,1)S(1)} %divide_convert_fusion), channel_id=1, source_target_pairs={{0,4},{4,8},{8,12},{12,16},{16,20},{20,24},{24,28},{28,32},{32,36}... | collective-permute-start | bytes 393224 | tf_op jit(solution)/shard_map/ppermute | solution.py:16
Sparse Core Ops, SparseCore 0:
  285.6 46.9 all-reduce.3
  344.6 44.5 all-gather.2
where the time goes:
time: 417 us; the launch traced here: 416 us
  blocking collectives  282 us (68%)
  waiting for transfers between devices  43.7 us (10%)
  other arithmetic  36.3 us (9%)
  local copies, waits for them, and re-layouts  19 us (5%)
  between operations  13.6 us (3%)
  matrix products  12.6 us (3%)
  starting transfers between devices  7.84 us (2%)
    psum x1, blocking collectives, local(): query_feats = lax.psum(contrib, ('tm', 'space')).astype(jnp.bfloat16)  250 us
    all_gather x1, waiting for transfers between devices, local(): lax.all_gather(carried[None], 'tm', axis=0, tiled=True)  26.2 us
    all_gather x1, blocking collectives, local(): lax.all_gather(retain_prod[None], 'tm', axis=0, tiled=True)  18.6 us
    select_n x16, other arithmetic, fold_step(): return jnp.where(source < position_tm, advanced, running)  18.4 us
    exp x1, local copies, waits for them, and re-layouts, local(): weights_exp = jnp.exp(scores - highest[:, None])  15.7 us
    psum x1, waiting for transfers between devices, local(): lax.psum((factor * totals, factor[..., None] * pos_sum, factor[..., None]...  15.6 us
    dot_general x1, matrix products, local(): jnp.dot(weights_exp.astype(jnp.bfloat16), frame_map, preferred_element_ty...  8.38 us
  transfers between devices with their start and end apart: 4, of which 4 were waited for; matrix products, arithmetic and copies ran while one was open for 6% of the time, Pallas kernels for 0%

commit v1 on v0

--- a/solution.py
+++ b/solution.py
@@ -3,6 +3,13 @@
 import jax.numpy as jnp
 from jax import lax
 from jax.sharding import PartitionSpec as P
+
+
+def swapped_in(shard, name, d):
+    size = lax.axis_size(name)
+    tiles = jnp.stack([shard for _ in range(size)])
+    tiles = lax.all_to_all(tiles, name, split_axis=0, concat_axis=0)
+    return jnp.concatenate(tiles, axis=d)
 
 
 def with_halo(cells, sides, width):
@@ -99,7 +106,7 @@
     local_prods.append(retain_prod)
     all_prods, all_ends = (
         lax.all_gather(retain_prod[None], "tm", axis=0, tiled=True),
-        lax.all_gather(carried[None], "tm", axis=0, tiled=True),
+        swapped_in(carried[None], "tm", 0),
     )
     position_tm = lax.axis_index("tm")
 

time: 417 us -> 488 us (1.17)
  blocking collectives: 282 us -> 368 us
  waiting for transfers between devices: 43.7 us -> 17.6 us
  starting transfers between devices: 7.84 us -> 17.3 us
    all_gather x1, blocking collectives: 18.6 us -> 104 us  [local(): lax.all_gather(retain_prod[None], 'tm', axis=0, tiled=True)]
    all_gather x1 -> x0, waiting for transfers between devices: 26.2 us -> none  [local(): lax.all_gather(carried[None], 'tm', axis=0, tiled=True)]
    all_to_all x0 -> x1, starting transfers between devices: none -> 9.52 us  [swapped_in(): tiles = lax.all_to_all(tiles, name, split_axis=0, concat_axis=0)]
  transfers between devices with their start and end apart: 4 -> 4, of which waited for: 4 -> 3; matrix products, arithmetic and copies ran while one was open for 6% -> 5% of each run, Pallas kernels for 0% -> 0%
where the time goes in v1:
time: 488 us; the launch traced here: 487 us
  blocking collectives  368 us (75%)
  other arithmetic  36.4 us (7%)
  local copies, waits for them, and re-layouts  21.4 us (4%)
  waiting for transfers between devices  17.6 us (4%)
  starting transfers between devices  17.3 us (4%)
  between operations  13.6 us (3%)
  matrix products  11.9 us (2%)
    psum x1, blocking collectives, local(): query_feats = lax.psum(contrib, ('tm', 'space')).astype(jnp.bfloat16)  250 us
    all_gather x1, blocking collectives, local(): lax.all_gather(retain_prod[None], 'tm', axis=0, tiled=True)  104 us
    select_n x16, other arithmetic, fold_step(): return jnp.where(source < position_tm, advanced, running)  18.4 us
    exp x1, local copies, waits for them, and re-layouts, local(): weights_exp = jnp.exp(scores - highest[:, None])  15.7 us
    psum x1, waiting for transfers between devices, local(): lax.psum((factor * totals, factor[..., None] * pos_sum, factor[..., None]...  15.6 us
  transfers between devices with their start and end apart: 4, of which 3 were waited for; matrix products, arithmetic and copies ran while one was open for 5% of the time, Pallas kernels for 0%

profile of v1, /device:TPU:1, one launch (start us, length us, event | category | flops | bytes accessed | tf_op | source)
XLA Modules:
  0.0 487.0 jit_solution(1266831229400419627)
XLA Ops:
  8.1 3.1 gather_fusion
  11.4 250.4 %all-reduce.5 = bf16[512,128]{1,0:T(8,128)(2,1)S(1)} all-reduce(f32[512,128]{1,0:T(8,128)S(1)} %convert_select_fusion), channel_id=1, replica_groups=mesh['video'=4,'tm'=16,'space'=4] {'tm','space'}, use_global_device_ids=true, to_apply=%region_0.1 | all-reduce | flops 65536 | bytes 393216 | tf_op jit(solution)/shard_map/psum | solution.py:52
  261.8 2.3 multiply_reduce_fusion
  264.1 7.0 %fusion.50 = (f32[512]{0:T(512)S(1)}, f32[512,7680]{1,0:T(8,128)}) fusion(f32[512]{0:T(512)S(1)} %get-tuple-element.139, f32[512,7680]{1,0:T(8,128)S(1)} %get-tuple-element.140), kind=kLoop, calls=%fused_computation.74 | loop fusion | flops 11795968 | bytes 31461376 | tf_op jit(solution)/shard_map/reduce_sum | solution.py:70
  271.1 6.0 %pmax.7 = f32[1,512]{1,0:T(1,128)S(1)} all-reduce(f32[1,512]{1,0:T(1,128)S(1)} %bitcast.67), channel_id=1, replica_groups=mesh['video'=4,'tm'=16,'space'=4] {'space'}, use_global_device_ids=true, to_apply=%region_2.3 | all-reduce | flops 512 | bytes 4096 | tf_op jit(solution)/shard_map/pmax | solution.py:82
  277.1 8.4 %fusion.7 = f32[1,512,128]{2,1,0:T(8,128)} fusion(bf16[7680,128]{1,0:T(8,128)(2,1)S(1)} %bitcast.63, f32[512,7680]{1,0:T(8,128)} %get-tuple-element.135, f32[512]{0:T(512)S(1)} %bitcast.65), kind=kOutput, calls=%fused_computation.11 | convolution fusion | flops 1010630656 | bytes 17958912 | tf_op jit(solution)/shard_map/dot_general | solution.py:76
  285.5 15.7 %copy.10 = f32[512,7680]{0,1:T(8,128)} copy(f32[512,7680]{1,0:T(8,128)} %get-tuple-element.135) | data formatting | bytes 31457280 | tf_op jit(solution)/shard_map/exp | solution.py:68
  301.2 7.9 %fusion.48 = (f32[512,240]{0,1:T(8,128)S(1)}, f32[512,32]{0,1:T(8,128)S(1)}) fusion(f32[512,32,240]{0,2,1:T(8,128)} %bitcast.64), kind=kLoop, calls=%fused_computation.72 | loop fusion | flops 7725056 | bytes 16285696 | tf_op jit(solution)/shard_map/reduce_sum | solution.py:72
  309.4 7.5 %all-reduce = (f32[512]{0:T(512)S(1)}, f32[1,512,2]{1,2,0:T(2,128)S(1)}) all-reduce(f32[512]{0:T(512)S(1)} %bitcast.71, f32[1,512,2]{1,2,0:T(2,128)S(1)} %maximum_multiply_fusion), channel_id=1, replica_groups=mesh['video'=4,'tm'=16,'space'=4] {'space'}, use_global_device_ids=true, to_apply=%region_9.10 | all-reduce | flops 1536 | bytes 12288 | tf_op jit(solution)/shard_map/psum | solution.py:84
  316.9 15.6 %all-reduce.4.cloned.1.call-done = f32[1,512,128]{2,1,0:T(8,128)} async-done(((f32[1,512,128]{2,1,0:T(8,128)}), f32[1,512,128]{2,1,0:T(8,128)}) %all-reduce.4.cloned.1.call-update) | async-done | bytes 262160 | tf_op jit(solution)/shard_map/psum | solution.py:84
  333.7 4.7 collective-permute-start.1
  338.4 3.1 collective-permute-start
  342.2 1.2 collective-permute-done
  343.8 2.4 stack.26
  346.2 9.5 %all-to-all-start = ((f32[16,1,512,128]{3,2,1,0:T(8,128)}), f32[16,1,512,128]{3,2,1,0:T(8,128)}, u32[]{:S(2)}, u32[]{:S(2)}) async-start(f32[16,1,512,128]{3,2,1,0:T(8,128)} %stack.26), calls=%async_computation | async-start | bytes 8388608 | tf_op jit(solution)/shard_map/all_to_all | solution.py:11
  355.7 104.4 %all-gather = f32[16,1,128]{2,1,0:T(1,128)S(1)} all-gather(f32[1,1,128]{2,1,0:T(1,128)S(1)} %bitcast.74), channel_id=1, replica_groups=mesh['video'=4,'tm'=16,'space'=4] {'tm'}, dimensions={0}, use_global_device_ids=true | all-gather | bytes 8704 | tf_op jit(solution)/shard_map/all_gather | solution.py:108
  460.1 19.0 %while.14 = (s32[]{:T(128)}, f32[512,128]{1,0:T(8,128)S(1)}, s32[]{:T(128)}, f32[16,128]{1,0:T(8,128)S(1)}, f32[16,512,128]{2,1,0:T(8,128)}, /*index=5*/s32[]{:T(128)}, s32[]{:T(128)}) while((s32[]{:T(128)}, f32[512,128]{1,0:T(8,128)S(1)}, s32[]{:T(128)}, f32[16,128]{1,0:T(8,128)S(1)}, f32[16,512,128]{2,1,0:T(8,128)}, ...), condition=%wide.region_12.13_spmd.clone, body=%wide.region_11.12_spmd.clone.sunk | while | flops 262148 | bytes 788081 | solution.py:117
  460.1 1.1 fusion.57
  461.3 1.1 fusion.57
  462.5 1.1 fusion.57
  463.7 1.1 fusion.57
  464.9 1.1 fusion.57
  466.1 1.1 fusion.57
  467.3 1.1 fusion.57
  468.5 1.1 fusion.57
  469.7 1.1 fusion.57
  470.8 1.1 fusion.57
  472.0 1.1 fusion.57
  473.2 1.1 fusion.57
  474.4 1.1 fusion.57
  475.6 1.1 fusion.57
  476.8 1.1 fusion.57
  (49 shorter events, 6.4 us)
Async XLA Ops:
  6.5 1.6 copy-start
  6.5 326.1 %all-reduce.4.cloned.1.call-start = ((), (), s32[]{:S(2)}) async-start(), calls=%async_computation.1 | async-start | bytes 524288 | tf_op jit(solution)/shard_map/psum | solution.py:84
  301.2 8.1 %copy-start.1 = (f32[1,128]{1,0:T(1,128)S(1)}, f32[1,128]{1,0:T(1,128)}, u32[]{:S(2)}) copy-start(f32[1,128]{1,0:T(1,128)} %param.14) | copy-start | bytes 1540
  301.2 15.7 %copy-start.2 = (f32[3,128]{1,0:T(4,128)S(1)}, f32[3,128]{1,0:T(4,128)}, u32[]{:S(2)}) copy-start(f32[3,128]{1,0:T(4,128)} %param.15) | copy-start | bytes 4612
  301.2 42.3 %copy-start.4 = (bf16[128,128]{1,0:T(8,128)(2,1)S(1)}, bf16[128,128]{1,0:T(8,128)(2,1)}, u32[]{:S(2)}) copy-start(bf16[128,128]{1,0:T(8,128)(2,1)} %param.16) | copy-start | bytes 98308
  301.2 177.9 %copy-start.3 = (f32[2,128]{1,0:T(2,128)S(1)}, f32[2,128]{1,0:T(2,128)}, u32[]{:S(2)}) copy-start(f32[2,128]{1,0:T(2,128)} %param.17) | copy-start | bytes 3076
  333.7 8.5 %collective-permute-start.1 = (bf16[1,512,128]{2,1,0:T(8,128)(2,1)S(1)}, bf16[1,512,128]{2,1,0:T(8,128)(2,1)S(1)}, u32[]{:S(2)}, u32[]{:S(2)}) collective-permute-start(bf16[1,512,128]{2,1,0:T(8,128)(2,1)S(1)} %divide_convert_fusion), channel_id=1, source_target_pairs={{4,0},{8,4},{12,8},{16,12},{20,16},{24,20},{28,24},{32,28},{36,32}... | collective-permute-start | bytes 393224 | tf_op jit(solution)/shard_map/ppermute | solution.py:25
  338.4 5.0 %collective-permute-start = (bf16[1,512,128]{2,1,0:T(8,128)(2,1)S(1)}, bf16[1,512,128]{2,1,0:T(8,128)(2,1)S(1)}, u32[]{:S(2)}, u32[]{:S(2)}) collective-permute-start(bf16[1,512,128]{2,1,0:T(8,128)(2,1)S(1)} %divide_convert_fusion), channel_id=1, source_target_pairs={{0,4},{4,8},{8,12},{12,16},{16,20},{20,24},{24,28},{28,32},{32,36}... | collective-permute-start | bytes 393224 | tf_op jit(solution)/shard_map/ppermute | solution.py:23
  346.2 114.0 %all-to-all-start = ((f32[16,1,512,128]{3,2,1,0:T(8,128)}), f32[16,1,512,128]{3,2,1,0:T(8,128)}, u32[]{:S(2)}, u32[]{:S(2)}) async-start(f32[16,1,512,128]{3,2,1,0:T(8,128)} %stack.26), calls=%async_computation | async-start | bytes 8388608 | tf_op jit(solution)/shard_map/all_to_all | solution.py:11
Sparse Core Ops, SparseCore 0:
  285.6 46.9 all-reduce.3
